TPU v7x, 512 devices: a whole 4x4x16 slice. The times are simulated.
512 devices in a mesh: gx: 16 (over z), gy: 32 (over x, y, core).
Axes of the slice: x: 4, y: 4, z: 16, core: 2. Of those that a mesh axis runs over, the one named last changes fastest.
Arguments:
- labels: int32 [64, 256, 128], P('gx', 'gy'), may hold values from 0 to 16, as said below
- layer_index: int32 [128], replicated, may hold values from 0 to 7
- layer_eps: float32 [8], replicated, may hold values from 1 to 12
Outputs:
- solution_block: float32 [16, 64, 256, 128], P(None, 'gx', 'gy')
- residual_block: float32 [16, 64, 256, 128], P(None, 'gx', 'gy')
Inputs may be any that keep to these rules, and one draw needn't show every extreme that they name: `labels`: 0 marks a dielectric cell; k marks a cell of conductor k.
All inputs are finite; a program needn't handle non-finite values.
Results may differ from a plain program's by a relative error of at most 0.0003.
Values sent between devices are 32-bit elements; how exact they have to be, the bound alone decides.
No kernel may reach another device: no remote copies, remote signals or barrier semaphores. Data moves between devices by JAX's collectives and lax.ppermute only.
A program may use at most 64 MiB of HBM per device.

v0:
```python
import jax
import jax.numpy as jnp
from jax import lax
from jax.sharding import PartitionSpec as P

K = 16
ITERS = 3


def extended(block, sides, width):
    for axis, dim in sides:
        count = lax.axis_size(axis)
        forward = [(i, i + 1) for i in range(count - 1)]
        backward = [(target, source) for source, target in forward]
        low = lax.ppermute(
            lax.slice_in_dim(block, block.shape[dim] - width, None, axis=dim), axis, forward
        )
        high = lax.ppermute(lax.slice_in_dim(block, 0, width, axis=dim), axis, backward)
        block = jnp.concatenate([low, block, high], axis=dim)
    return block


def coefficients(layer_index, layer_eps):
    table = (
        layer_index[:, None] == jnp.arange(layer_eps.shape[0], dtype=jnp.int32)[None, :]
    ).astype(jnp.float32)
    eps_plane = jnp.dot(
        table, layer_eps, precision=lax.Precision.HIGHEST, preferred_element_type=jnp.float32
    )
    middle = 0.5 * (eps_plane[1:] + eps_plane[:-1])
    c_down = jnp.concatenate([eps_plane[:1], middle])
    c_up = jnp.concatenate([middle, eps_plane[-1:]])
    diagonal = 4.0 * eps_plane + c_down + c_up
    return (eps_plane, c_down, c_up, diagonal)


def laplace(padded, coeffs):
    eps_plane, c_down, c_up, diagonal = coeffs
    field = padded[:, 1:-1, 1:-1]
    lateral = (
        padded[:, 2:, 1:-1] + padded[:, :-2, 1:-1] + padded[:, 1:-1, 2:] + padded[:, 1:-1, :-2]
    )
    below = jnp.pad(field[..., :-1], ((0, 0), (0, 0), (0, 0), (1, 0)))
    above = jnp.pad(field[..., 1:], ((0, 0), (0, 0), (0, 0), (0, 1)))
    return diagonal * field - eps_plane * lateral - c_down * below - c_up * above


def local_gram(left, right):
    count = left.shape[0]
    return jnp.dot(
        left.reshape(count, -1),
        right.reshape(count, -1).T,
        precision=lax.Precision.HIGHEST,
        preferred_element_type=jnp.float32,
    )


def combine_rows(coef, field):
    count = field.shape[0]
    return jnp.dot(
        coef,
        field.reshape(count, -1),
        precision=lax.Precision.HIGHEST,
        preferred_element_type=jnp.float32,
    ).reshape(field.shape)


def lower_inverse(factor):
    count = factor.shape[0]
    inverse = jnp.zeros((count, count), jnp.float32)
    unit = jnp.eye(count, dtype=jnp.float32)
    for row in range(count):
        partial_row = unit[row] - jnp.dot(factor[row], inverse, precision=lax.Precision.HIGHEST)
        inverse = inverse.at[row].set(partial_row / factor[row, row])
    return inverse


def apply_operator(search, free, coeffs):
    padded = extended(search, (("gx", 1), ("gy", 2)), 1)
    return free * laplace(padded, coeffs)


def on_device(labels, layer_index, layer_eps):
    coeffs = coefficients(layer_index, layer_eps)
    free = (labels == 0).astype(jnp.float32)
    conductor_ids = jnp.arange(1, K + 1, dtype=jnp.int32)
    excitation = (labels[None] == conductor_ids[:, None, None, None]).astype(jnp.float32)
    padded_exc = extended(excitation, (("gx", 1), ("gy", 2)), 1)
    right_side = -free * laplace(padded_exc, coeffs)
    inverse_diag = free / coeffs[3]
    solution = jnp.zeros_like(right_side)
    residual = right_side
    prev_search = None
    prev_image = None
    for step in range(ITERS):
        precond = inverse_diag * residual
        if step == 0:
            search = precond
        else:
            beta = lax.psum(local_gram(prev_image, precond), ("gx", "gy"))
            search = precond - combine_rows(beta.T, prev_search)
        image = apply_operator(search, free, coeffs)
        curvature = lax.psum(local_gram(search, image), ("gx", "gy"))
        inverse = lower_inverse(jnp.linalg.cholesky(curvature))
        prev_search = combine_rows(inverse, search)
        prev_image = combine_rows(inverse, image)
        alpha = lax.psum(local_gram(prev_search, residual), ("gx", "gy"))
        solution = solution + combine_rows(alpha.T, prev_search)
        residual = residual - combine_rows(alpha.T, prev_image)
    return (solution, residual)


def solution(mesh):
    placed = (P("gx", "gy", None), P(), P())
    return jax.shard_map(
        on_device,
        mesh=mesh,
        in_specs=placed,
        out_specs=(P(None, "gx", "gy", None), P(None, "gx", "gy", None)),
        check_vma=False,
    )
```

profile of v0, /device:TPU:1, one launch (start us, length us, event | category | flops | bytes accessed | tf_op | source)
XLA Modules:
  0.0 967.6 jit_solution(16897844907388868109)
XLA Ops:
  1.5 4.4 collective-permute-start.1
  11.1 6.7 collective-permute-start.2
  17.8 1.9 collective-permute-start.3
  21.2 1.9 collective-permute-start.5
  24.5 5.3 collective-permute-done.4
  29.8 2.3 collective-permute-start.6
  32.1 4.7 collective-permute-start.7
  38.8 113.6 %psum.56 = f32[16,16]{0,1:T(8,128)S(1)} all-reduce(f32[16,16]{0,1:T(8,128)S(1)} %convolution_bitcast_fusion.7), channel_id=1, replica_groups=mesh['gx'=16,'gy'=32] {'gx','gy'}, use_global_device_ids=true, to_apply=%region_0.1 | all-reduce | flops 256 | bytes 2048 | tf_op jit(solution)/shard_map/psum | solution.py:103
  170.9 1.5 fusion.72
  179.8 98.8 %psum.57 = f32[16,16]{1,0:T(8,128)S(1)} all-reduce(f32[16,16]{1,0:T(8,128)S(1)} %fusion.176), channel_id=1, replica_groups=mesh['gx'=16,'gy'=32] {'gx','gy'}, use_global_device_ids=true, to_apply=%region_3.5 | all-reduce | flops 256 | bytes 2048 | tf_op jit(solution)/shard_map/psum | solution.py:107
  279.7 99.6 %psum.58 = f32[16,16]{1,0:T(8,128)S(1)} all-reduce(f32[16,16]{1,0:T(8,128)S(1)} %fusion.170), channel_id=1, replica_groups=mesh['gx'=16,'gy'=32] {'gx','gy'}, use_global_device_ids=true, to_apply=%region_4.6 | all-reduce | flops 256 | bytes 2048 | tf_op jit(solution)/shard_map/psum | solution.py:100
  379.8 2.8 collective-permute-start.9
  384.1 3.6 collective-permute-done.8
  387.7 4.0 collective-permute-start.10
  391.7 2.5 collective-permute-start.11
  396.2 104.3 %psum.59 = f32[16,16]{0,1:T(8,128)S(1)} all-reduce(f32[16,16]{0,1:T(8,128)S(1)} %convolution_bitcast_fusion.6), channel_id=1, replica_groups=mesh['gx'=16,'gy'=32] {'gx','gy'}, use_global_device_ids=true, to_apply=%region_5.7 | all-reduce | flops 256 | bytes 2048 | tf_op jit(solution)/shard_map/psum | solution.py:103
  528.1 98.5 %psum.60 = f32[16,16]{1,0:T(8,128)S(1)} all-reduce(f32[16,16]{1,0:T(8,128)S(1)} %fusion.164), channel_id=1, replica_groups=mesh['gx'=16,'gy'=32] {'gx','gy'}, use_global_device_ids=true, to_apply=%region_6.8 | all-reduce | flops 256 | bytes 2048 | tf_op jit(solution)/shard_map/psum | solution.py:107
  627.7 100.0 %psum.61 = f32[16,16]{1,0:T(8,128)S(1)} all-reduce(f32[16,16]{1,0:T(8,128)S(1)} %fusion.158), channel_id=1, replica_groups=mesh['gx'=16,'gy'=32] {'gx','gy'}, use_global_device_ids=true, to_apply=%region_7.9 | all-reduce | flops 256 | bytes 2048 | tf_op jit(solution)/shard_map/psum | solution.py:100
  728.2 2.6 collective-permute-start.13
  732.6 3.3 collective-permute-done.12
  735.9 4.0 collective-permute-start.14
  739.9 2.6 collective-permute-start.15
  744.6 104.5 %psum.62 = f32[16,16]{0,1:T(8,128)S(1)} all-reduce(f32[16,16]{0,1:T(8,128)S(1)} %convolution_bitcast_fusion.5), channel_id=1, replica_groups=mesh['gx'=16,'gy'=32] {'gx','gy'}, use_global_device_ids=true, to_apply=%region_8.10 | all-reduce | flops 256 | bytes 2048 | tf_op jit(solution)/shard_map/psum | solution.py:103
  866.7 98.5 %psum.63 = f32[16,16]{1,0:T(8,128)S(1)} all-reduce(f32[16,16]{1,0:T(8,128)S(1)} %fusion.152), channel_id=1, replica_groups=mesh['gx'=16,'gy'=32] {'gx','gy'}, use_global_device_ids=true, to_apply=%region_9.11 | all-reduce | flops 256 | bytes 2048 | tf_op jit(solution)/shard_map/psum | solution.py:107
  (205 shorter events, 94.4 us)
Async XLA Ops:
  0.6 6.6 copy-start
  1.5 5.7 copy-start.6
  1.5 8.2 collective-permute-start.1
  5.9 5.2 collective-permute-start
  8.1 1.5 copy-start.1
  11.1 8.6 collective-permute-start.2
  17.8 3.1 collective-permute-start.3
  21.2 3.2 collective-permute-start.5
  23.1 6.6 collective-permute-start.4
  24.4 132.3 %copy-start.2 = (f32[16,16]{1,0:T(8,128)}, f32[16,16]{1,0:T(8,128)S(1)}, u32[]{:S(2)}) copy-start(f32[16,16]{1,0:T(8,128)S(1)} %fusion.220) | copy-start | bytes 3076
  29.8 7.1 collective-permute-start.6
  32.1 5.9 collective-permute-start.7
  155.3 1.4 copy-start.4
  379.8 4.3 collective-permute-start.9
  382.6 5.0 collective-permute-start.8
  387.7 6.9 collective-permute-start.10
  391.7 3.6 collective-permute-start.11
  503.4 1.4 copy-start.5
  503.4 0.7 copy-start.3
  728.2 4.3 collective-permute-start.13
  730.8 5.0 collective-permute-start.12
  735.9 6.8 collective-permute-start.14
  739.9 3.8 collective-permute-start.15
where the time goes:
time: 971 us; the launch traced here: 968 us
  blocking collectives  818 us (84%)
  matrix products  66.8 us (7%)
  starting transfers between devices  45.5 us (5%)
  waiting for transfers between devices  17.5 us (2%)
  other arithmetic  12.7 us (1%)
    psum x3, blocking collectives, on_device(): curvature = lax.psum(local_gram(search, image), ('gx', 'gy'))  322 us
    psum x3, blocking collectives, on_device(): alpha = lax.psum(local_gram(prev_search, residual), ('gx', 'gy'))  296 us
    psum x2, blocking collectives, on_device(): beta = lax.psum(local_gram(prev_image, precond), ('gx', 'gy'))  200 us
    dot_general x48, matrix products, lower_inverse(): jnp.dot(factor[row], inverse, precision=lax.Precision.HIGHEST)  55.8 us
    ppermute x8, starting transfers between devices, extended(): lax.ppermute(lax.slice_in_dim(block, block.shape[dim] - width, None, axis...  23.4 us
    ppermute x8, starting transfers between devices, extended(): lax.ppermute(lax.slice_in_dim(block, 0, width, axis=dim), axis, backward)  22.1 us
  transfers between devices with their start and end apart: 16, of which 8 were waited for; matrix products, arithmetic and copies ran while one was open for 0% of the time, Pallas kernels for 0%

commit v1 on v0

--- a/solution.py
+++ b/solution.py
@@ -97,7 +97,7 @@
         if step == 0:
             search = precond
         else:
-            beta = lax.psum(local_gram(prev_image, precond), ("gx", "gy"))
+            beta = jnp.sum(lax.all_gather(local_gram(prev_image, precond), ("gx", "gy")), axis=0)
             search = precond - combine_rows(beta.T, prev_search)
         image = apply_operator(search, free, coeffs)
         curvature = lax.psum(local_gram(search, image), ("gx", "gy"))

time: 971 us -> 1070 us (1.10)
  blocking collectives: 818 us -> 909 us
  waiting for transfers between devices: 17.5 us -> 5.99 us
    all_gather x0 -> x2, blocking collectives: none -> 285 us  [on_device(): lax.all_gather(local_gram(prev_image, precond), ('gx', 'gy'))]
    psum x2 -> x0, blocking collectives: 200 us -> none  [on_device(): beta = lax.psum(local_gram(prev_image, precond), ('gx', 'gy'))]
    ppermute x8, waiting for transfers between devices: 13.5 us -> 0.13 us  [extended(): lax.ppermute(lax.slice_in_dim(block, 0, width, axis=dim), axis, backward)]
  transfers between devices with their start and end apart: 16 -> 16, of which waited for: 8 -> 8; matrix products, arithmetic and copies ran while one was open for 0% -> 1% of each run, Pallas kernels for 0% -> 0%
where the time goes in v1:
time: 1070 us; the launch traced here: 1060 us
  blocking collectives  909 us (85%)
  matrix products  67 us (6%)
  starting transfers between devices  50.7 us (5%)
  other arithmetic  19.6 us (2%)
    psum x3, blocking collectives, on_device(): curvature = lax.psum(local_gram(search, image), ('gx', 'gy'))  322 us
    psum x3, blocking collectives, on_device(): alpha = lax.psum(local_gram(prev_search, residual), ('gx', 'gy'))  302 us
    all_gather x2, blocking collectives, on_device(): lax.all_gather(local_gram(prev_image, precond), ('gx', 'gy'))  285 us
    dot_general x48, matrix products, lower_inverse(): jnp.dot(factor[row], inverse, precision=lax.Precision.HIGHEST)  55.9 us
    ppermute x8, starting transfers between devices, extended(): lax.ppermute(lax.slice_in_dim(block, block.shape[dim] - width, None, axis...  27.7 us
    ppermute x8, starting transfers between devices, extended(): lax.ppermute(lax.slice_in_dim(block, 0, width, axis=dim), axis, backward)  23.1 us
  transfers between devices with their start and end apart: 16, of which 8 were waited for; matrix products, arithmetic and copies ran while one was open for 1% of the time, Pallas kernels for 0%

profile of v1, /device:TPU:1, one launch (start us, length us, event | category | flops | bytes accessed | tf_op | source)
XLA Modules:
  0.0 1061.6 jit_solution(6266094457406896427)
XLA Ops:
  2.8 5.0 collective-permute-start.1
  11.6 8.3 collective-permute-start.2
  20.0 1.9 collective-permute-start.3
  25.3 4.0 collective-permute-start.5
  30.7 3.2 collective-permute-start.6
  33.9 4.1 collective-permute-start.7
  39.8 113.5 %psum.42 = f32[16,16]{0,1:T(8,128)S(1)} all-reduce(f32[16,16]{0,1:T(8,128)S(1)} %convolution_bitcast_fusion.5), channel_id=1, replica_groups=mesh['gx'=16,'gy'=32] {'gx','gy'}, use_global_device_ids=true, to_apply=%region_0.1 | all-reduce | flops 256 | bytes 2048 | tf_op jit(solution)/shard_map/psum | solution.py:103
  168.8 1.5 fusion.68
  180.7 100.7 %psum.43 = f32[16,16]{1,0:T(8,128)S(1)} all-reduce(f32[16,16]{1,0:T(8,128)S(1)} %fusion.176), channel_id=1, replica_groups=mesh['gx'=16,'gy'=32] {'gx','gy'}, use_global_device_ids=true, to_apply=%region_3.5 | all-reduce | flops 256 | bytes 2048 | tf_op jit(solution)/shard_map/psum | solution.py:107
  282.7 142.4 %all-gather = f32[8192,16]{1,0:T(8,128)} all-gather(f32[16,16]{1,0:T(8,128)S(1)} %fusion.170), channel_id=2, replica_groups=mesh['gx'=16,'gy'=32] {'gx','gy'}, dimensions={0}, use_global_device_ids=true | all-gather | bytes 525312 | tf_op jit(solution)/shard_map/all_gather | solution.py:100
  425.1 2.7 reduce_sum.18
  429.8 4.0 collective-permute-start.9
  435.1 3.2 collective-permute-start.10
  438.3 2.4 collective-permute-start.11
  442.5 104.4 %psum.44 = f32[16,16]{0,1:T(8,128)S(1)} all-reduce(f32[16,16]{0,1:T(8,128)S(1)} %convolution_bitcast_fusion.4), channel_id=1, replica_groups=mesh['gx'=16,'gy'=32] {'gx','gy'}, use_global_device_ids=true, to_apply=%region_5.7 | all-reduce | flops 256 | bytes 2048 | tf_op jit(solution)/shard_map/psum | solution.py:103
  562.5 1.5 fusion.100
  574.4 100.8 %psum.45 = f32[16,16]{1,0:T(8,128)S(1)} all-reduce(f32[16,16]{1,0:T(8,128)S(1)} %fusion.164), channel_id=1, replica_groups=mesh['gx'=16,'gy'=32] {'gx','gy'}, use_global_device_ids=true, to_apply=%region_6.8 | all-reduce | flops 256 | bytes 2048 | tf_op jit(solution)/shard_map/psum | solution.py:107
  676.5 142.3 %all-gather.1 = f32[8192,16]{1,0:T(8,128)} all-gather(f32[16,16]{1,0:T(8,128)S(1)} %fusion.158), channel_id=3, replica_groups=mesh['gx'=16,'gy'=32] {'gx','gy'}, dimensions={0}, use_global_device_ids=true | all-gather | bytes 525312 | tf_op jit(solution)/shard_map/all_gather | solution.py:100
  818.8 2.7 reduce_sum.19
  823.4 4.0 collective-permute-start.13
  828.7 3.2 collective-permute-start.14
  831.9 2.4 collective-permute-start.15
  836.1 104.4 %psum.46 = f32[16,16]{0,1:T(8,128)S(1)} all-reduce(f32[16,16]{0,1:T(8,128)S(1)} %convolution_bitcast_fusion.3), channel_id=1, replica_groups=mesh['gx'=16,'gy'=32] {'gx','gy'}, use_global_device_ids=true, to_apply=%region_8.10 | all-reduce | flops 256 | bytes 2048 | tf_op jit(solution)/shard_map/psum | solution.py:103
  958.4 100.6 %psum.47 = f32[16,16]{1,0:T(8,128)S(1)} all-reduce(f32[16,16]{1,0:T(8,128)S(1)} %fusion.152), channel_id=1, replica_groups=mesh['gx'=16,'gy'=32] {'gx','gy'}, use_global_device_ids=true, to_apply=%region_9.11 | all-reduce | flops 256 | bytes 2048 | tf_op jit(solution)/shard_map/psum | solution.py:107
  (213 shorter events, 97.1 us)
Async XLA Ops:
  0.6 7.2 copy-start
  1.5 10.1 collective-permute-start
  2.8 8.8 collective-permute-start.1
  11.6 11.0 %collective-permute-start.2 = (f32[16,6,1,128]{3,0,2,1:T(8,128)S(1)}, f32[16,6,1,128]{3,0,2,1:T(8,128)S(1)}, u32[]{:S(2)}, u32[]{:S(2)}) collective-permute-start(f32[16,6,1,128]{3,0,2,1:T(8,128)S(1)} %get-tuple-element.600), channel_id=1, source_target_pairs={{1,0},{2,1},{3,2},{4,3},{5,4},{6,5},{7,6},{8,7},{9,8},{10,9},{11,1... | collective-permute-start | bytes 147464 | tf_op jit(solution)/shard_map/ppermute | solution.py:18
  20.0 3.1 collective-permute-start.3
  24.0 5.4 collective-permute-start.4
  25.3 5.3 collective-permute-start.5
  29.3 129.1 %copy-start.1 = (f32[16,16]{1,0:T(8,128)}, f32[16,16]{1,0:T(8,128)S(1)}, u32[]{:S(2)}) copy-start(f32[16,16]{1,0:T(8,128)S(1)} %fusion.218) | copy-start | bytes 3076
  30.7 7.6 collective-permute-start.6
  33.9 5.2 collective-permute-start.7
  156.2 2.3 copy-start.3
  427.9 122.7 %copy-start.2 = (f32[16,16]{1,0:T(8,128)S(1)}, f32[16,16]{1,0:T(8,128)}, u32[]{:S(2)}) copy-start(f32[16,16]{1,0:T(8,128)} %copy-done.1) | copy-start | bytes 3076
  428.5 5.4 collective-permute-start.8
  429.8 5.3 collective-permute-start.9
  435.1 6.2 collective-permute-start.10
  438.3 3.5 collective-permute-start.11
  549.8 2.3 copy-start.4
  822.1 5.7 collective-permute-start.12
  823.4 5.3 collective-permute-start.13
  828.7 5.9 collective-permute-start.14
  831.9 3.5 collective-permute-start.15

commit v2 on v0

--- a/solution.py
+++ b/solution.py
@@ -100,7 +100,7 @@
             beta = lax.psum(local_gram(prev_image, precond), ("gx", "gy"))
             search = precond - combine_rows(beta.T, prev_search)
         image = apply_operator(search, free, coeffs)
-        curvature = lax.psum(local_gram(search, image), ("gx", "gy"))
+        curvature = lax.psum(lax.psum(local_gram(search, image), "gy"), "gx")
         inverse = lower_inverse(jnp.linalg.cholesky(curvature))
         prev_search = combine_rows(inverse, search)
         prev_image = combine_rows(inverse, image)

time: 971 us -> 938 us (0.966)
  blocking collectives: 818 us -> 786 us
    psum x3 -> x6, blocking collectives: 322 us -> 264 us  [on_device(): curvature = lax.psum(lax.psum(local_gram(search, image), 'gy'), 'gx')]
    psum x3, blocking collectives: 296 us -> 318 us  [on_device(): alpha = lax.psum(local_gram(prev_search, residual), ('gx', 'gy'))]
where the time goes in v2:
time: 938 us; the launch traced here: 934 us
  blocking collectives  786 us (84%)
  matrix products  67 us (7%)
  starting transfers between devices  44.1 us (5%)
  waiting for transfers between devices  17.5 us (2%)
  other arithmetic  12.7 us (1%)
    psum x3, blocking collectives, on_device(): alpha = lax.psum(local_gram(prev_search, residual), ('gx', 'gy'))  318 us
    psum x6, blocking collectives, on_device(): curvature = lax.psum(lax.psum(local_gram(search, image), 'gy'), 'gx')  264 us
    psum x2, blocking collectives, on_device(): beta = lax.psum(local_gram(prev_image, precond), ('gx', 'gy'))  203 us
    dot_general x48, matrix products, lower_inverse(): jnp.dot(factor[row], inverse, precision=lax.Precision.HIGHEST)  56 us
    ppermute x8, starting transfers between devices, extended(): lax.ppermute(lax.slice_in_dim(block, 0, width, axis=dim), axis, backward)  22.1 us
    ppermute x8, starting transfers between devices, extended(): lax.ppermute(lax.slice_in_dim(block, block.shape[dim] - width, None, axis...  22 us
  transfers between devices with their start and end apart: 16, of which 8 were waited for; matrix products, arithmetic and copies ran while one was open for 0% of the time, Pallas kernels for 0%

profile of v2, /device:TPU:1, one launch (start us, length us, event | category | flops | bytes accessed | tf_op | source)
XLA Modules:
  0.0 934.3 jit_solution(5239269594201794985)
XLA Ops:
  1.5 4.4 collective-permute-start.1
  11.1 6.7 collective-permute-start.2
  17.8 1.9 collective-permute-start.3
  21.2 1.9 collective-permute-start.5
  24.5 5.3 collective-permute-done.4
  29.8 2.3 collective-permute-start.6
  32.1 4.7 collective-permute-start.7
  38.8 64.4 %psum.77 = f32[16,16]{0,1:T(8,128)S(1)} all-reduce(f32[16,16]{0,1:T(8,128)S(1)} %convolution_bitcast_fusion.7), channel_id=1, replica_groups=mesh['gx'=16,'gy'=32] {'gy'}, use_global_device_ids=true, to_apply=%region_0.1 | all-reduce | flops 256 | bytes 2048 | tf_op jit(solution)/shard_map/psum | solution.py:103
  103.3 27.8 %psum.78 = f32[16,16]{0,1:T(8,128)S(1)} all-reduce(f32[16,16]{0,1:T(8,128)S(1)} %psum.77), channel_id=1, replica_groups=mesh['gx'=16,'gy'=32] {'gx'}, use_global_device_ids=true, to_apply=%region_1.2 | all-reduce | flops 256 | bytes 2048 | tf_op jit(solution)/shard_map/psum | solution.py:103
  158.5 106.9 %psum.79 = f32[16,16]{1,0:T(8,128)S(1)} all-reduce(f32[16,16]{1,0:T(8,128)S(1)} %fusion.176), channel_id=1, replica_groups=mesh['gx'=16,'gy'=32] {'gx','gy'}, use_global_device_ids=true, to_apply=%region_4.6 | all-reduce | flops 256 | bytes 2048 | tf_op jit(solution)/shard_map/psum | solution.py:107
  266.5 101.6 %psum.80 = f32[16,16]{1,0:T(8,128)S(1)} all-reduce(f32[16,16]{1,0:T(8,128)S(1)} %fusion.170), channel_id=1, replica_groups=mesh['gx'=16,'gy'=32] {'gx','gy'}, use_global_device_ids=true, to_apply=%region_5.7 | all-reduce | flops 256 | bytes 2048 | tf_op jit(solution)/shard_map/psum | solution.py:100
  371.9 3.6 collective-permute-done.8
  375.5 4.0 collective-permute-start.10
  379.5 2.8 collective-permute-start.11
  384.4 62.3 %psum.81 = f32[16,16]{0,1:T(8,128)S(1)} all-reduce(f32[16,16]{0,1:T(8,128)S(1)} %convolution_bitcast_fusion.6), channel_id=1, replica_groups=mesh['gx'=16,'gy'=32] {'gy'}, use_global_device_ids=true, to_apply=%region_6.8 | all-reduce | flops 256 | bytes 2048 | tf_op jit(solution)/shard_map/psum | solution.py:103
  446.7 23.7 %psum.82 = f32[16,16]{0,1:T(8,128)S(1)} all-reduce(f32[16,16]{0,1:T(8,128)S(1)} %psum.81), channel_id=1, replica_groups=mesh['gx'=16,'gy'=32] {'gx'}, use_global_device_ids=true, to_apply=%region_7.9 | all-reduce | flops 256 | bytes 2048 | tf_op jit(solution)/shard_map/psum | solution.py:103
  498.0 105.6 %psum.83 = f32[16,16]{1,0:T(8,128)S(1)} all-reduce(f32[16,16]{1,0:T(8,128)S(1)} %fusion.164), channel_id=1, replica_groups=mesh['gx'=16,'gy'=32] {'gx','gy'}, use_global_device_ids=true, to_apply=%region_8.10 | all-reduce | flops 256 | bytes 2048 | tf_op jit(solution)/shard_map/psum | solution.py:107
  604.7 101.6 %psum.84 = f32[16,16]{1,0:T(8,128)S(1)} all-reduce(f32[16,16]{1,0:T(8,128)S(1)} %fusion.158), channel_id=1, replica_groups=mesh['gx'=16,'gy'=32] {'gx','gy'}, use_global_device_ids=true, to_apply=%region_9.11 | all-reduce | flops 256 | bytes 2048 | tf_op jit(solution)/shard_map/psum | solution.py:100
  710.4 3.3 collective-permute-done.12
  713.7 4.0 collective-permute-start.14
  717.7 2.8 collective-permute-start.15
  722.6 62.3 %psum.85 = f32[16,16]{0,1:T(8,128)S(1)} all-reduce(f32[16,16]{0,1:T(8,128)S(1)} %convolution_bitcast_fusion.5), channel_id=1, replica_groups=mesh['gx'=16,'gy'=32] {'gy'}, use_global_device_ids=true, to_apply=%region_10.12 | all-reduce | flops 256 | bytes 2048 | tf_op jit(solution)/shard_map/psum | solution.py:103
  784.9 23.7 %psum.86 = f32[16,16]{0,1:T(8,128)S(1)} all-reduce(f32[16,16]{0,1:T(8,128)S(1)} %psum.85), channel_id=1, replica_groups=mesh['gx'=16,'gy'=32] {'gx'}, use_global_device_ids=true, to_apply=%region_11.13 | all-reduce | flops 256 | bytes 2048 | tf_op jit(solution)/shard_map/psum | solution.py:103
  826.3 105.6 %psum.87 = f32[16,16]{1,0:T(8,128)S(1)} all-reduce(f32[16,16]{1,0:T(8,128)S(1)} %fusion.152), channel_id=1, replica_groups=mesh['gx'=16,'gy'=32] {'gx','gy'}, use_global_device_ids=true, to_apply=%region_12.14 | all-reduce | flops 256 | bytes 2048 | tf_op jit(solution)/shard_map/psum | solution.py:107
  (208 shorter events, 99.7 us)
Async XLA Ops:
  0.6 6.6 copy-start
  1.5 5.7 copy-start.6
  1.5 8.2 collective-permute-start.1
  5.9 5.2 collective-permute-start
  8.1 1.5 copy-start.1
  11.1 8.6 collective-permute-start.2
  17.8 3.1 collective-permute-start.3
  21.2 3.2 collective-permute-start.5
  23.1 6.6 collective-permute-start.4
  24.4 110.9 %copy-start.2 = (f32[16,16]{1,0:T(8,128)}, f32[16,16]{1,0:T(8,128)S(1)}, u32[]{:S(2)}) copy-start(f32[16,16]{1,0:T(8,128)S(1)} %fusion.220) | copy-start | bytes 3076
  29.8 7.1 collective-permute-start.6
  32.1 5.9 collective-permute-start.7
  133.9 1.5 copy-start.4
  368.7 3.2 collective-permute-start.9
  370.4 5.0 collective-permute-start.8
  375.5 7.3 collective-permute-start.10
  379.5 4.0 collective-permute-start.11
  473.2 1.5 copy-start.5
  473.3 0.7 copy-start.3
  706.9 3.5 collective-permute-start.13
  708.6 5.0 collective-permute-start.12
  713.7 7.0 collective-permute-start.14
  717.7 4.0 collective-permute-start.15
